TPU v7x, 512 devices: a whole 4x8x8 slice. The times are simulated.
512 devices in a mesh: row: 16 (over z, core), col: 32 (over x, y).
Axes of the slice: x: 4, y: 8, z: 8, core: 2. Of those that a mesh axis runs over, the one named last changes fastest.
Arguments:
- strip: float32 [20480, 128], P('row'), may hold values from -6 to 6
- block_below: float32 [64, 64], replicated, may hold values from -1 to 1
- inverse_first: float32 [64, 64], replicated, may hold values from -0.5 to 1.5, as said below
- inverse_second: float32 [64, 64], replicated, may hold values from -0.5 to 1.5, as said below
- cotangent: float32 [20480, 20480], P('row', 'col'), may hold values from -0.0390625 to 0.0390625
Outputs:
- strip_grad: float32 [20480, 128], P('row')
Inputs may be any that keep to these rules, and one draw needn't show every extreme that they name: inverse_first is lower triangular with its diagonal in 0.5 to 1.5. inverse_second is lower triangular with its diagonal in 0.5 to 1.5.
All inputs are finite; a program needn't handle non-finite values.
Results may differ from a plain program's by a relative error of at most 0.00007.
Values sent between devices are 32-bit elements; how exact they have to be, the bound alone decides.
A program may use at most 64 MiB of HBM per device.

v0:
```python
import jax
import jax.numpy as jnp
from jax import lax
from jax.sharding import PartitionSpec as P


def from_root(value, axis, source):
    kept = jnp.where(lax.axis_index(axis) == source, value, 0).astype(value.dtype)
    return lax.psum(kept, axis)


def mul(left, right):
    return jnp.dot(left, right, precision=lax.Precision.HIGHEST, preferred_element_type=jnp.float32)


def finish(bar_sum, left_block, inverse_first, inverse_second, panel):
    bar_updated = mul(-bar_sum[:, panel:], inverse_second)
    bar_first = -bar_sum[:, :panel] - mul(bar_updated, left_block)
    return jnp.concatenate([mul(bar_first, inverse_first), bar_updated], axis=1)


def shards(strip, block_below, inverse_first, inverse_second, cotangent):
    panel = inverse_first.shape[0]
    cols_here = cotangent.shape[1]
    ratio = lax.axis_size("col") // lax.axis_size("row")
    col_id = lax.axis_index("col")
    owner = col_id // ratio
    offset = col_id % ratio * cols_here
    lower_first = mul(strip[:, :panel], inverse_first.T)
    left_block = mul(block_below, inverse_first.T)
    updated = strip[:, panel:] - mul(lower_first, left_block.T)
    col_first = from_root(lax.dynamic_slice_in_dim(lower_first, offset, cols_here, 0), "row", owner)
    lower_second = mul(updated, inverse_second.T)
    col_second = from_root(
        lax.dynamic_slice_in_dim(lower_second, offset, cols_here, 0), "row", owner
    )
    col_lower = jnp.concatenate([col_first, col_second], axis=1)
    lower = jnp.concatenate([lower_first, lower_second], axis=1)
    transposed = lax.dot_general(
        cotangent,
        lower,
        (((0,), (0,)), ((), ())),
        precision=lax.Precision.HIGHEST,
        preferred_element_type=jnp.float32,
    )
    col_total = lax.psum(transposed, "row")
    row_index = lax.axis_index("row")
    pieces = []
    for member in range(ratio):
        pieces.append(from_root(col_total, "col", row_index * ratio + member))
    routed = jnp.concatenate(pieces, axis=0)
    local_sum = mul(cotangent, col_lower)
    row_total = lax.psum(local_sum, "col")
    row_total = row_total + routed
    return finish(row_total, left_block, inverse_first, inverse_second, panel)


def solution(mesh):
    return jax.shard_map(
        shards,
        mesh=mesh,
        in_specs=(P("row", None), P(), P(), P(), P("row", "col")),
        out_specs=P("row", None),
        check_vma=False,
    )
```

profile of v0, /device:TPU:1, one launch (start us, length us, event | category | flops | bytes accessed | tf_op | source)
XLA Modules:
  0.0 318.0 jit_solution(9730919756724847951)
XLA Ops:
  6.5 0.0 copy-start
  6.5 0.0 all-reduce.7.cloned.1.call-start
  6.5 1.1 fusion.11
  7.7 2.7 fusion.3
  10.3 0.0 copy-start.1
  10.3 2.5 convolution_subtract_fusion
  12.8 1.6 fusion.12
  14.5 0.0 copy-done
  14.5 3.8 %convolution_bitcast_fusion.1 = f32[640,128]{0,1:T(8,128)} fusion(f32[1280,640]{1,0:T(8,128)S(1)} %copy-done, f32[1280,64]{0,1:T(8,128)S(1)} %fusion.12, f32[1280,64]{0,1:T(8,128)} %fusion.3), kind=kOutput, calls=%fused_computation.3 | convolution fusion | flops 1258455040 | bytes 4259840 | tf_op jit(solution)/shard_map/dot_general | solution.py:39
  18.3 0.0 copy-done.1
  18.3 0.7 dynamic-slice_select_fusion
  19.1 0.0 all-reduce.7.cloned.1.call-update
  19.1 0.0 all-reduce.5.cloned.1.call-start
  19.1 122.2 %all-reduce.7.cloned.1.call-done = (f32[640,64]{0,1:T(8,128)}, f32[640,64]{0,1:T(8,128)}, f32[640,128]{0,1:T(8,128)}) async-done(((f32[640,64]{0,1:T(8,128)}, f32[640,64]{0,1:T(8,128)}, f32[640,128]{0,1:T(8,128)}), (f32[640,64]{0,1:T(8,128)}, f32[640,64]{0,1:T(8,128)}, f32[640,128]{0,1:T(8,128)})) %all-reduce.7.cloned.1.call-update) | async-done | bytes 655376 | tf_op jit(solution)/shard_map/psum | solution.py:9
  141.3 0.0 copy-start.2
  141.3 0.0 copy-start.4
  141.3 5.3 %convolution_bitcast_fusion = f32[1280,128]{0,1:T(8,128)} fusion(f32[1280,640]{1,0:T(8,128)S(1)} %copy-done, f32[640,64]{0,1:T(8,128)} %get-tuple-element.8, f32[640,64]{0,1:T(8,128)} %get-tuple-element.9), kind=kOutput, calls=%fused_computation.1 | convolution fusion | flops 1258373120 | bytes 4259840 | tf_op jit(solution)/shard_map/dot_general | solution.py:13
  146.7 0.0 copy-start.3
  146.7 0.0 copy-done.2
  146.7 0.9 broadcast_select_fusion.1
  147.5 0.0 all-reduce.5.cloned.1.call-update
  147.6 157.7 %all-reduce.5.cloned.1.call-done = (f32[1280,128]{0,1:T(8,128)}, f32[640,128]{0,1:T(8,128)}, f32[640,128]{0,1:T(8,128)}) async-done(((f32[1280,128]{0,1:T(8,128)}, f32[640,128]{0,1:T(8,128)}, f32[640,128]{0,1:T(8,128)}), (f32[1280,128]{0,1:T(8,128)}, f32[640,128]{0,1:T(8,128)}, f32[640,128]{0,1:T(8,128)})) %all-reduce.5.cloned.1.call-update) | async-done | bytes 1310736 | tf_op jit(solution)/shard_map/psum | solution.py:53
  305.3 1.3 maximum_add_fusion
  306.6 0.0 copy-done.4
  306.6 0.5 fusion.5
  307.1 0.5 convolution_subtract_fusion.1
  307.6 0.0 copy-done.3
  307.6 0.5 fusion.13
  308.1 0.9 pad_maximum_fusion
  309.0 2.2 copy.6
Async XLA Ops:
  6.5 7.9 %copy-start = (f32[1280,640]{1,0:T(8,128)S(1)}, f32[1280,640]{1,0:T(8,128)}, u32[]{:S(2)}) copy-start(f32[1280,640]{1,0:T(8,128)} %param.9) | copy-start | bytes 9830404
  6.5 134.8 %all-reduce.7.cloned.1.call-start = ((), (), s32[]{:S(2)}) async-start(), calls=%async_computation.1 | async-start | bytes 1310720 | tf_op jit(solution)/shard_map/psum | solution.py:9
  10.3 8.0 %copy-start.1 = (f32[1280,64]{0,1:T(8,128)S(1)}, f32[1280,64]{0,1:T(8,128)}, u32[]{:S(2)}) copy-start(f32[1280,64]{0,1:T(8,128)} %fusion.3) | copy-start | bytes 983044
  19.1 286.2 %all-reduce.5.cloned.1.call-start = ((), (), s32[]{:S(2)}) async-start(), calls=%async_computation | async-start | bytes 2621440 | tf_op jit(solution)/shard_map/psum | solution.py:53
  141.3 5.3 %copy-start.2 = (f32[640,128]{0,1:T(8,128)S(1)}, f32[640,128]{0,1:T(8,128)}, u32[]{:S(2)}) copy-start(f32[640,128]{0,1:T(8,128)} %get-tuple-element.10) | copy-start | bytes 983044
  141.3 165.3 %copy-start.4 = (f32[64,64]{1,0:T(8,128)S(1)}, f32[64,64]{1,0:T(8,128)}, u32[]{:S(2)}) copy-start(f32[64,64]{1,0:T(8,128)} %param.8) | copy-start | bytes 49156
  146.7 160.9 %copy-start.3 = (f32[64,64]{1,0:T(8,128)S(1)}, f32[64,64]{1,0:T(8,128)}, u32[]{:S(2)}) copy-start(f32[64,64]{1,0:T(8,128)} %param.7) | copy-start | bytes 49156
Sparse Core Ops, SparseCore 0:
  19.2 122.0 all-reduce.6
  147.7 157.5 all-reduce.4
where the time goes:
time: 321 us; the launch traced here: 318 us
  waiting for transfers between devices  280 us (87%)
  matrix products  18.5 us (6%)
  between operations  13.5 us (4%)
  other arithmetic  3.85 us (1%)
    psum x1, waiting for transfers between devices, shards(): row_total = lax.psum(local_sum, 'col')  158 us
    psum x1, waiting for transfers between devices, from_root(): return lax.psum(kept, axis)  122 us
    dot_general x8, matrix products, mul(): jnp.dot(left, right, precision=lax.Precision.HIGHEST, preferred_element_t...  14.6 us
  transfers between devices with their start and end apart: 2, of which 2 were waited for; matrix products, arithmetic and copies ran while one was open for 0% of the time, Pallas kernels for 0%

commit v1 on v0

v1 whole, which is shorter than its diff:
```python
import jax
import jax.numpy as jnp
from jax import lax
from jax.experimental import pallas as pl
from jax.experimental.pallas import tpu as pltpu
from jax.sharding import PartitionSpec as P

MESH = pl.DeviceIdType.MESH
NX, NY, NZ, NC = 4, 8, 8, 2
ROWS, COLS, STRIP, PANEL = 1280, 640, 128, 64
PART = ROWS // NX
SUB = PART // NY
PIECE = COLS // NX // NC
Y_FAR = (4, 3, 5, 2, 6, 1, 7)
Y_NEAR = (1, 7, 2, 6, 3, 5, 4)
X_FAR = (2, 1, 3)
Z_FAR = (4, 3, 5, 2, 6, 1, 7)
C_CHUNKS = 5


def exact(left, right, dims=((1,), (0,))):
    return lax.dot_general(
        left, right, (dims, ((), ())),
        precision=lax.Precision.HIGHEST, preferred_element_type=jnp.float32,
    )


def halves(value):
    high = value.astype(jnp.bfloat16)
    low = (value - high.astype(jnp.float32)).astype(jnp.bfloat16)
    return high, low


def rows_of(start, size):
    return pl.ds(pl.multiple_of(start, 8), size)


def kernel(
    strip_h, below_h, first_h, second_h, cot_h, out_h,
    strip_v, below_v, first_v, second_v, cot_v, split_v, lower_v, column_v, relay_v,
    weights_v, back_v, backs_v, backsum_v, backin_v,
    part_v, xin_v, ysend_v, yin_v, out_v, unit_v,
    load_sem, store_sem, peer_sem,
    s1, r1, s2, r2, s3, r3, sb, rb, sf, rf, sx, rx, sy, ry, syg, ryg, sxg, rxg,
):
    row, col = lax.axis_index("row"), lax.axis_index("col")
    z, c = row // NC, row % NC
    x, y = col // NY, col % NY

    def at(z_, c_, x_, y_):
        return (z_ * NC + c_, x_ * NY + y_)

    def send(src, dst, ssem, rsem, device):
        copy = pltpu.make_async_remote_copy(
            src_ref=src, dst_ref=dst, send_sem=ssem, recv_sem=rsem,
            device_id=device, device_id_type=MESH,
        )
        copy.start()
        return copy

    def arrived(dst, rsem):
        pltpu.make_async_copy(dst, dst, rsem).wait()

    def turn(base, d, n):
        return lax.rem(base + d, n)

    barrier = pltpu.get_barrier_semaphore()
    peers = []
    for d in range(1, NX):
        peers += [at(z, c, turn(x, d, NX), y), at(z, 1 - c, turn(x, d, NX), y)]
    for d in range(1, NY):
        peers.append(at(z, c, x, turn(y, d, NY)))
    for d in range(1, NZ):
        peers += [at(turn(z, d, NZ), c, x, y), at(turn(z, d, NZ), 1 - c, x, y)]
    peers.append(at(z, 1 - c, x, y))
    for peer in peers:
        pl.semaphore_signal(barrier, inc=1, device_id=peer, device_id_type=MESH)

    small = []
    for i, (src, dst) in enumerate(((below_h, below_v), (first_h, first_v), (second_h, second_v), (strip_h, strip_v))):
        copy = pltpu.make_async_copy(src, dst, load_sem.at[i])
        copy.start()
        small.append(copy)
    chunk = ROWS // C_CHUNKS
    loads = []
    for i in range(C_CHUNKS):
        rows = pl.ds(i * chunk, chunk)
        copy = pltpu.make_async_copy(cot_h.at[rows], cot_v.at[rows], load_sem.at[4 + i])
        copy.start()
        loads.append(copy)

    for copy in small[:3]:
        copy.wait()
    first, second = first_v[...], second_v[...]
    left = exact(below_v[...], first, ((1,), (1,)))
    mixed = exact(exact(second, left), first)
    unit_v[0:PANEL, 0:PANEL] = first
    unit_v[0:PANEL, PANEL:] = jnp.zeros_like(first)
    unit_v[PANEL:, 0:PANEL] = -mixed
    unit_v[PANEL:, PANEL:] = second
    small[3].wait()
    lower_v[...] = exact(strip_v[...], unit_v[...], ((1,), (1,)))

    pl.semaphore_wait(barrier, len(peers))
    for d in range(1, NX):
        pl.semaphore_signal(peer_sem, inc=1, device_id=at(z, c, turn(x, d, NX), y), device_id_type=MESH)

    is_source = (y // 2) == lax.rem(row, NX)
    target_x = row // NX
    source_rows = lax.rem(y, 2) * COLS
    in_plane = (2 * x + y // NX) == z
    has_block = jnp.logical_and(in_plane, lax.rem(y // 2, NC) == c)

    @pl.when(is_source)
    def _():
        for i, d in enumerate(Z_FAR):
            for h in range(NC):
                src = lower_v.at[rows_of(source_rows + (x * NC + h) * PIECE, PIECE)]
                send(src, relay_v.at[target_x], s1.at[i * NC + h], r1.at[target_x], at(turn(z, d, NZ), h, x, y))

    @pl.when(has_block)
    def _():
        send(lower_v.at[rows_of(source_rows, COLS)], column_v, s3.at[0], r3.at[0], at(z, 1 - c, x, y))
        column_v[...] = lower_v[rows_of(source_rows, COLS), :]

    for i in range(C_CHUNKS):
        loads[i].wait()
        rows = pl.ds(i * chunk, chunk)
        high, low = halves(cot_v[rows, :])
        split_v[rows, 0:COLS] = high
        split_v[rows, COLS:] = low

    high, low = halves(jnp.transpose(lower_v[...]))
    back = jnp.dot(jnp.concatenate([high, low], axis=0), split_v[...], preferred_element_type=jnp.float32)
    back = back[0:STRIP] + back[STRIP:]
    back_v[...] = jnp.transpose(back[:, 0:COLS] + back[:, COLS:])
    pl.semaphore_wait(peer_sem, NX - 1)
    mine = z * NC + (1 - c)
    for d in (4, 3, 5, 2, 6, 1, 7, 0):
        for e in range(NC):
            if d == 0 and e == 0:
                continue
            z_, c_ = turn(z, d, NZ), lax.rem(c + e, NC)
            src = back_v.at[rows_of((z_ * NC + 1 - c_) * SUB, SUB)]
            k = d * NC + e
            send(src, backs_v.at[k], sb.at[k], rb.at[k], at(z_, c_, x, y))

    for d in (1, 3, 2, 0):
        x_ = turn(x, d, NX)

        @pl.when((2 * x_ + y // NX) != z)
        def _(d=d, x_=x_):
            arrived(relay_v.at[x_], r1.at[x_])
            here = rows_of((x * NC + c) * PIECE, PIECE)
            for e in range(NC):
                if d == 0 and e == 0:
                    column_v[here, :] = relay_v[x_]
                    continue
                k = d * NC + e
                send(relay_v.at[x_], column_v.at[here], s2.at[k], r2.at[x * NC + c], at(z, lax.rem(c + e, NC), x_, y))

    @pl.when(jnp.logical_not(in_plane))
    def _():
        for d in range(NX):
            for e in range(NC):
                if d == 0 and e == 0:
                    continue
                k = turn(x, d, NX) * NC + lax.rem(c + e, NC)
                arrived(column_v.at[rows_of(k * PIECE, PIECE)], r2.at[k])

    @pl.when(jnp.logical_and(in_plane, jnp.logical_not(has_block)))
    def _():
        arrived(column_v, r3.at[0])

    high, low = halves(column_v[...])
    both = jnp.concatenate([high, low], axis=1)
    weights_v[0:COLS, :] = both
    weights_v[COLS:, :] = both
    for d in X_FAR + (0,):
        x_ = turn(x, d, NX)
        part = jnp.dot(
            split_v[pl.ds(pl.multiple_of(x_ * PART, 16), PART), :], weights_v[...],
            preferred_element_type=jnp.float32,
        )
        part_v[rows_of(x_ * PART, PART), :] = part[:, 0:STRIP] + part[:, STRIP:]
        if d:
            for e in Y_FAR + (0,):
                y_ = turn(y, e, NY)
                src = part_v.at[rows_of(x_ * PART + y_ * SUB, SUB)]
                k = (d - 1) * NY + e
                send(src, xin_v.at[d - 1, e], sx.at[k], rx.at[k], at(z, c, x_, y))

    total = back_v[rows_of(mine * SUB, SUB), :]
    for k in range(1, NZ * NC):
        arrived(backs_v.at[k], rb.at[k])
        total = total + backs_v[k]
    backsum_v[...] = total
    send(backsum_v, backin_v, sf.at[0], rf.at[0], (col // 2, lax.rem(col, 2) * (NZ * NC) + mine))

    kept = None
    for e in Y_FAR + (0,):
        y_ = turn(y, e, NY)
        total = part_v[rows_of(x * PART + y_ * SUB, SUB), :]
        for d in range(1, NX):
            k = (d - 1) * NY + e
            arrived(xin_v.at[d - 1, e], rx.at[k])
            total = total + xin_v[d - 1, e]
        if e:
            ysend_v[e] = total
            send(ysend_v.at[e], yin_v.at[e], sy.at[e], ry.at[e], at(z, c, x, y_))
        else:
            kept = total
    for e in range(1, NY):
        arrived(yin_v.at[e], ry.at[e])
        kept = kept + yin_v[e]
    arrived(backin_v, rf.at[0])
    kept = kept + backin_v[...]

    here = rows_of(x * PART + y * SUB, SUB)
    out_v[here, :] = -exact(kept, unit_v[...])
    for e in Y_FAR:
        send(out_v.at[here], out_v.at[here], syg.at[e], ryg.at[e], at(z, c, x, turn(y, e, NY)))

    for e in (0,) + Y_NEAR:
        y_ = turn(y, NY - e, NY)
        block = out_v.at[rows_of(x * PART + y_ * SUB, SUB)]
        if e:
            arrived(block, ryg.at[e])
        for d in X_FAR:
            k = (d - 1) * NY + e
            send(block, block, sxg.at[k], rxg.at[k], at(z, c, turn(x, d, NX), y))

    stores = []
    for d in (0, 1, 3, 2):
        x_ = turn(x, NX - d, NX)
        rows = rows_of(x_ * PART, PART)
        if d:
            for e in range(NY):
                y_ = turn(y, NY - e, NY)
                arrived(out_v.at[rows_of(x_ * PART + y_ * SUB, SUB)], rxg.at[(d - 1) * NY + e])
        copy = pltpu.make_async_copy(out_v.at[rows], out_h.at[rows], store_sem.at[d])
        copy.start()
        stores.append(copy)

    def left_here(ref, sem):
        pltpu.make_async_copy(ref, ref, sem).wait()

    @pl.when(is_source)
    def _():
        for i in range((NZ - 1) * NC):
            left_here(relay_v.at[0], s1.at[i])

    @pl.when(has_block)
    def _():
        left_here(column_v, s3.at[0])

    for d in range(NX):
        x_ = turn(x, d, NX)

        @pl.when((2 * x_ + y // NX) != z)
        def _(d=d):
            for e in range(NC):
                if d or e:
                    left_here(relay_v.at[0], s2.at[d * NC + e])

    for k in range(1, NZ * NC):
        left_here(backs_v.at[k], sb.at[k])
    left_here(backsum_v, sf.at[0])
    for k in range((NX - 1) * NY):
        left_here(backsum_v, sx.at[k])
        left_here(backsum_v, sxg.at[k])
    for e in range(1, NY):
        left_here(backsum_v, sy.at[e])
        left_here(backsum_v, syg.at[e])
    for copy in stores:
        copy.wait()


def shards(strip, below, first, second, cotangent):
    f32, bf16 = jnp.float32, jnp.bfloat16
    dma = pltpu.SemaphoreType.DMA
    pairs = (
        (NZ - 1) * NC, NX, NX * NC, NX * NC, 1, 1, NZ * NC, NZ * NC, 1, 1,
        (NX - 1) * NY, (NX - 1) * NY, NY, NY, NY, NY, (NX - 1) * NY, (NX - 1) * NY,
    )
    return pl.pallas_call(
        kernel,
        out_shape=jax.ShapeDtypeStruct((ROWS, STRIP), f32),
        in_specs=[pl.BlockSpec(memory_space=pl.ANY)] * 5,
        out_specs=pl.BlockSpec(memory_space=pl.ANY),
        scratch_shapes=[
            pltpu.VMEM((ROWS, STRIP), f32),
            pltpu.VMEM((PANEL, PANEL), f32),
            pltpu.VMEM((PANEL, PANEL), f32),
            pltpu.VMEM((PANEL, PANEL), f32),
            pltpu.VMEM((ROWS, COLS), f32),
            pltpu.VMEM((ROWS, 2 * COLS), bf16),
            pltpu.VMEM((ROWS, STRIP), f32),
            pltpu.VMEM((COLS, STRIP), f32),
            pltpu.VMEM((NX, PIECE, STRIP), f32),
            pltpu.VMEM((2 * COLS, 2 * STRIP), bf16),
            pltpu.VMEM((COLS, STRIP), f32),
            pltpu.VMEM((NZ * NC, SUB, STRIP), f32),
            pltpu.VMEM((SUB, STRIP), f32),
            pltpu.VMEM((SUB, STRIP), f32),
            pltpu.VMEM((ROWS, STRIP), f32),
            pltpu.VMEM((NX - 1, NY, SUB, STRIP), f32),
            pltpu.VMEM((NY, SUB, STRIP), f32),
            pltpu.VMEM((NY, SUB, STRIP), f32),
            pltpu.VMEM((ROWS, STRIP), f32),
            pltpu.VMEM((STRIP, STRIP), f32),
            dma((4 + C_CHUNKS,)),
            dma((NX,)),
            pltpu.SemaphoreType.REGULAR,
        ] + [dma((n,)) for n in pairs],
        compiler_params=pltpu.CompilerParams(
            collective_id=0, has_side_effects=True, vmem_limit_bytes=40 << 20,
        ),
    )(strip, below, first, second, cotangent)


def solution(mesh):
    return jax.shard_map(
        shards,
        mesh=mesh,
        in_specs=(P("row", None), P(), P(), P(), P("row", "col")),
        out_specs=P("row", None),
        check_vma=False,
    )
```

time: 321 us -> 67.1 us (0.21)
  waiting for transfers between devices: 280 us -> 0 us
  Pallas kernels: 0 us -> 60.5 us
  matrix products: 18.5 us -> 0 us
  between operations: 13.5 us -> 0.01 us
  local copies, waits for them, and re-layouts: 2.18 us -> 6.12 us
  other arithmetic: 3.85 us -> 0 us
    psum x2 -> x0, waiting for transfers between devices: 280 us -> none  [the longest x1 158 us: shards(): row_total = lax.psum(local_sum, 'col')]
    pallas_call x0 -> x1, Pallas kernels: none -> 60.5 us  [shards(): pl.pallas_call(kernel, out_shape=jax.ShapeDtypeStruct((ROWS, STRIP), f32)...]
    dot_general x9 -> x0, matrix products: 18.5 us -> none  [the longest x8 14.6 us: mul(): jnp.dot(left, right, precision=lax.Precision.HIGHEST, preferred_element_t...]
    unnamed x10 -> x11, local copies, waits for them, and re-layouts: 0.02 us -> 6.12 us
  transfers between devices with their start and end apart: 2 -> 0, of which waited for: 2 -> 0; matrix products, arithmetic and copies ran while one was open for 0% -> 0% of each run, Pallas kernels for 0% -> 0%
where the time goes in v1:
time: 67.1 us; the launch traced here: 66.7 us
  Pallas kernels  60.5 us (90%)
  local copies, waits for them, and re-layouts  6.12 us (9%)
    pallas_call x1, Pallas kernels, shards(): pl.pallas_call(kernel, out_shape=jax.ShapeDtypeStruct((ROWS, STRIP), f32)...  60.5 us
    unnamed x11, local copies, waits for them, and re-layouts  6.12 us

profile of v1, /device:TPU:1, one launch (start us, length us, event | category | flops | bytes accessed | tf_op | source)
XLA Modules:
  0.0 66.7 jit_solution(17767220168167661965)
XLA Ops:
  0.0 0.0 copy-start
  0.0 1.9 %copy-done = f32[1280,640]{1,0:T(8,128)S(1)} copy-done((f32[1280,640]{1,0:T(8,128)S(1)}, f32[1280,640]{1,0:T(8,128)}, u32[]{:S(2)}) %copy-start) | copy-done | bytes 3276824
  1.9 0.0 copy-start.1
  1.9 1.1 %copy-done.1 = f32[1280,128]{1,0:T(8,128)S(1)} copy-done((f32[1280,128]{1,0:T(8,128)S(1)}, f32[1280,128]{1,0:T(8,128)}, u32[]{:S(2)}) %copy-start.1) | copy-done | bytes 655384
  3.0 0.0 copy-start.2
  3.0 0.8 %copy-done.2 = f32[64,64]{1,0:T(8,128)S(1)} copy-done((f32[64,64]{1,0:T(8,128)S(1)}, f32[64,64]{1,0:T(8,128)}, u32[]{:S(2)}) %copy-start.2) | copy-done | bytes 16408
  3.8 0.0 copy-start.3
  3.8 0.8 %copy-done.3 = f32[64,64]{1,0:T(8,128)S(1)} copy-done((f32[64,64]{1,0:T(8,128)S(1)}, f32[64,64]{1,0:T(8,128)}, u32[]{:S(2)}) %copy-start.3) | copy-done | bytes 16408
  4.5 0.0 copy-start.4
  4.5 0.8 %copy-done.4 = f32[64,64]{1,0:T(8,128)S(1)} copy-done((f32[64,64]{1,0:T(8,128)S(1)}, f32[64,64]{1,0:T(8,128)}, u32[]{:S(2)}) %copy-start.4) | copy-done | bytes 16408
  5.3 60.5 %shard_map.55 = f32[1280,128]{1,0:T(8,128)S(1)} custom-call(f32[1280,128]{1,0:T(8,128)S(1)} %copy-done.1, f32[64,64]{1,0:T(8,128)S(1)} %copy-done.2, f32[64,64]{1,0:T(8,128)S(1)} %copy-done.3, f32[64,64]{1,0:T(8,128)S(1)} %copy-done.4, f32[1280,640]{1,0:T(8,128)S(1)} %copy-done), custom_call_target="tpu_custom_call" | custom-call | tf_op jit(solution)/shard_map/pallas_call | solution.py:286
  65.8 0.8 %copy.7 = f32[1280,128]{1,0:T(8,128)} copy(f32[1280,128]{1,0:T(8,128)S(1)} %shard_map.55) | data formatting | bytes 1310720
Async XLA Ops:
  0.0 1.9 %copy-start = (f32[1280,640]{1,0:T(8,128)S(1)}, f32[1280,640]{1,0:T(8,128)}, u32[]{:S(2)}) copy-start(f32[1280,640]{1,0:T(8,128)} %cot_h.1) | copy-start | bytes 9830404
  1.9 1.1 %copy-start.1 = (f32[1280,128]{1,0:T(8,128)S(1)}, f32[1280,128]{1,0:T(8,128)}, u32[]{:S(2)}) copy-start(f32[1280,128]{1,0:T(8,128)} %strip_h.1) | copy-start | bytes 1966084
  3.0 0.8 %copy-start.2 = (f32[64,64]{1,0:T(8,128)S(1)}, f32[64,64]{1,0:T(8,128)}, u32[]{:S(2)}) copy-start(f32[64,64]{1,0:T(8,128)} %below_h.1) | copy-start | bytes 49156
  3.8 0.8 %copy-start.3 = (f32[64,64]{1,0:T(8,128)S(1)}, f32[64,64]{1,0:T(8,128)}, u32[]{:S(2)}) copy-start(f32[64,64]{1,0:T(8,128)} %first_h.1) | copy-start | bytes 49156
  4.5 0.8 %copy-start.4 = (f32[64,64]{1,0:T(8,128)S(1)}, f32[64,64]{1,0:T(8,128)}, u32[]{:S(2)}) copy-start(f32[64,64]{1,0:T(8,128)} %second_h.1) | copy-start | bytes 49156

commit v2 on v1

v2 whole, which is shorter than its diff:
```python
import jax
import jax.numpy as jnp
from jax import lax
from jax.experimental import pallas as pl
from jax.experimental.pallas import tpu as pltpu
from jax.sharding import PartitionSpec as P

MESH = pl.DeviceIdType.MESH
NX, NY, NZ, NC = 4, 8, 8, 2
ROWS, COLS, STRIP, PANEL = 1280, 640, 128, 64
HALF = ROWS // 2
MAIN, REST = 32, 8
SUB = MAIN + REST
PART = MAIN * NY
EDGE = PART * 2
PIECE = COLS // NX // NC
Y_FAR = (4, 3, 5, 2, 6, 1, 7)
Y_NEAR = (1, 7, 2, 6, 3, 5, 4)
X_FAR = (2, 1, 3)
Z_FAR = (4, 3, 5, 2, 6, 1, 7)
C_CHUNKS = 5


def exact(left, right, dims=((1,), (0,))):
    return lax.dot_general(
        left, right, (dims, ((), ())),
        precision=lax.Precision.HIGHEST, preferred_element_type=jnp.float32,
    )


def halves(value):
    high = value.astype(jnp.bfloat16)
    low = (value - high.astype(jnp.float32)).astype(jnp.bfloat16)
    return high, low


def rows_of(start, size):
    return pl.ds(pl.multiple_of(start, 8), size)


def kernel(
    strip_h, below_h, first_h, second_h, cot_h, out_v,
    strip_v, below_v, first_v, second_v, cot_v, split_v, column_v, relay_v, weights_v,
    back_v, pairin_v, backs_v, backsum_v, backin_v,
    part_v, xin_v, ysend_v, yin_v, yin2_v, xsend2_v, xin2_v, unit_v,
    load_sem, peer_sem,
    s1, r1, s2, r2, s3, r3, sp, rp, sb, rb, sf, rf, sx, rx, sy, ry, syg, ryg, sxg, rxg,
    sy2, ry2, sx2, rx2, sxg2, rxg2, syg2, ryg2,
):
    row, col = lax.axis_index("row"), lax.axis_index("col")
    z, c = row // NC, row % NC
    x, y = col // NY, col % NY

    def at(z_, c_, x_, y_):
        return (z_ * NC + c_, x_ * NY + y_)

    def send(src, dst, ssem, rsem, device):
        copy = pltpu.make_async_remote_copy(
            src_ref=src, dst_ref=dst, send_sem=ssem, recv_sem=rsem,
            device_id=device, device_id_type=MESH,
        )
        copy.start()
        return copy

    def arrived(dst, rsem):
        pltpu.make_async_copy(dst, dst, rsem).wait()

    def turn(base, d, n):
        return lax.rem(base + d, n)

    barrier = pltpu.get_barrier_semaphore()
    peers = []
    for d in range(1, NX):
        peers += [at(z, c, turn(x, d, NX), y), at(z, 1 - c, turn(x, d, NX), y)]
    for d in range(1, NY):
        peers.append(at(z, c, x, turn(y, d, NY)))
    for d in range(1, NZ):
        peers += [at(turn(z, d, NZ), c, x, y), at(turn(z, d, NZ), 1 - c, x, y)]
    peers.append(at(z, 1 - c, x, y))
    for peer in peers:
        pl.semaphore_signal(barrier, inc=1, device_id=peer, device_id_type=MESH)

    small = []
    for i, (src, dst) in enumerate(((below_h, below_v), (first_h, first_v), (second_h, second_v), (strip_h, strip_v))):
        copy = pltpu.make_async_copy(src, dst, load_sem.at[i])
        copy.start()
        small.append(copy)
    chunk = ROWS // C_CHUNKS
    loads = []
    for i in range(C_CHUNKS):
        rows = pl.ds(i * chunk, chunk)
        copy = pltpu.make_async_copy(cot_h.at[rows], cot_v.at[rows], load_sem.at[4 + i])
        copy.start()
        loads.append(copy)

    pl.semaphore_wait(barrier, len(peers))
    for d in range(1, NX):
        pl.semaphore_signal(peer_sem, inc=1, device_id=at(z, c, turn(x, d, NX), y), device_id_type=MESH)

    is_source = (y // 2) == lax.rem(row, 4)
    target_x = row // 4
    source_rows = lax.rem(y, 2) * COLS
    in_plane = (2 * x + y // 4) == z
    has_block = jnp.logical_and(in_plane, lax.rem(y // 2, NC) == c)

    @pl.when(is_source)
    def _():
        for i, d in enumerate(Z_FAR):
            for h in range(NC):
                src = strip_h.at[rows_of(source_rows + (x * NC + h) * PIECE, PIECE)]
                send(src, relay_v.at[target_x], s1.at[i * NC + h], r1.at[target_x], at(turn(z, d, NZ), h, x, y))

    @pl.when(has_block)
    def _():
        send(strip_h.at[rows_of(source_rows, COLS)], column_v, s3.at[0], r3.at[0], at(z, 1 - c, x, y))

    for copy in small[:3]:
        copy.wait()
    first, second = first_v[...], second_v[...]
    left = exact(below_v[...], first, ((1,), (1,)))
    mixed = exact(exact(second, left), first)
    unit_v[0:PANEL, 0:PANEL] = first
    unit_v[0:PANEL, PANEL:] = jnp.zeros_like(first)
    unit_v[PANEL:, 0:PANEL] = -mixed
    unit_v[PANEL:, PANEL:] = second
    small[3].wait()

    for i in range(C_CHUNKS):
        loads[i].wait()
        rows = pl.ds(i * chunk, chunk)
        high, low = halves(cot_v[rows, :])
        split_v[rows, 0:COLS] = high
        split_v[rows, COLS:] = low

    high, low = halves(jnp.transpose(exact(strip_v[...], unit_v[...], ((1,), (1,)))))
    back = jnp.dot(jnp.concatenate([high, low], axis=0), split_v[...], preferred_element_type=jnp.float32)
    back = back[0:STRIP] + back[STRIP:]
    back = jnp.transpose(back[:, 0:COLS] + back[:, COLS:])
    pieces = NZ * NC
    for k in range(pieces):
        back_v[1 - k % 2, k // 2, 0:MAIN] = back[k * MAIN:(k + 1) * MAIN]
        rest = pieces * MAIN + (k % NY * 2 + k // NY) * REST
        back_v[1 - k % 2, k // 2, MAIN:] = back[rest:rest + REST]
    pl.semaphore_wait(peer_sem, NX - 1)
    send(back_v.at[1 - c], pairin_v, sp.at[0], rp.at[0], at(z, 1 - c, x, y))

    for d in (1, 3, 2, 0):
        x_ = turn(x, d, NX)

        @pl.when((2 * x_ + y // 4) != z)
        def _(d=d, x_=x_):
            arrived(relay_v.at[x_], r1.at[x_])
            here = rows_of((x * NC + c) * PIECE, PIECE)
            for e in range(NC):
                if d == 0 and e == 0:
                    column_v[here, :] = relay_v[x_]
                    continue
                k = d * NC + e
                send(relay_v.at[x_], column_v.at[here], s2.at[k], r2.at[x * NC + c], at(z, lax.rem(c + e, NC), x_, y))

    arrived(pairin_v, rp.at[0])
    back_v[c] = back_v[c] + pairin_v[...]
    for d in Z_FAR:
        z_ = turn(z, d, NZ)
        send(back_v.at[c, z_], backs_v.at[d], sb.at[d], rb.at[d], at(z_, c, x, y))

    @pl.when(has_block)
    def _():
        column_v[...] = strip_v[rows_of(source_rows, COLS), :]

    @pl.when(jnp.logical_and(in_plane, jnp.logical_not(has_block)))
    def _():
        arrived(column_v, r3.at[0])

    for d in (0, 1, 3, 2):
        x_ = turn(x, d, NX)

        @pl.when(jnp.logical_not(in_plane))
        def _(d=d, x_=x_):
            for e in range(NC):
                if d or e:
                    k = x_ * NC + lax.rem(c + e, NC)
                    arrived(column_v.at[rows_of(k * PIECE, PIECE)], r2.at[k])

        start, size = x_ * (NC * PIECE), NC * PIECE
        high, low = halves(exact(column_v[rows_of(start, size), :], unit_v[...], ((1,), (1,))))
        both = jnp.concatenate([high, low], axis=1)
        weights_v[pl.ds(pl.multiple_of(start, 32), size), :] = both
        weights_v[pl.ds(pl.multiple_of(COLS + start, 32), size), :] = both

    def product(start, size):
        part = jnp.dot(
            split_v[pl.ds(pl.multiple_of(start, 128), size), :], weights_v[...],
            preferred_element_type=jnp.float32,
        )
        return part[:, 0:STRIP] + part[:, STRIP:]

    for half in range(2):
        part_v[half, EDGE:HALF] = product(half * HALF + EDGE, HALF - EDGE)
    for e in Y_FAR:
        y_ = turn(y, e, NY)
        send(part_v.at[:, rows_of(EDGE + y_ * 2 * REST, 2 * REST)], yin2_v.at[e], sy2.at[e], ry2.at[e], at(z, c, x, y_))
    for d in X_FAR + (0,):
        x_ = turn(x, d, NX)
        half, start = x_ // 2, lax.rem(x_, 2) * PART
        part_v[half, rows_of(start, PART), :] = product(half * HALF + start, PART)
        if d:
            for e in Y_FAR + (0,):
                y_ = turn(y, e, NY)
                k = (d - 1) * NY + e
                send(part_v.at[half, rows_of(start + y_ * MAIN, MAIN)], xin_v.at[d - 1, e], sx.at[k], rx.at[k], at(z, c, x_, y))

    mine, low_x = x // 2, lax.rem(x, 2)
    kept = None
    for i, e in enumerate(Y_FAR + (0,)):
        if i == 3:
            total = back_v[c, z]
            for d in range(1, NZ):
                arrived(backs_v.at[d], rb.at[d])
                total = total + backs_v[d]
            backsum_v[...] = total
            target = lax.rem(col, 2) * pieces + z * NC + (1 - c)
            send(backsum_v, backin_v, sf.at[0], rf.at[0], (col // 2, target))
        if i == 6:
            total = part_v[:, rows_of(EDGE + y * 2 * REST, 2 * REST), :]
            for d in range(1, NY):
                arrived(yin2_v.at[d], ry2.at[d])
                total = total + yin2_v[d]
            xsend2_v[...] = total
            for d in X_FAR:
                x_ = turn(x, d, NX)
                src = xsend2_v.at[x_ // 2, rows_of(lax.rem(x_, 2) * REST, REST)]
                send(src, xin2_v.at[d], sx2.at[d], rx2.at[d], at(z, c, x_, y))
        y_ = turn(y, e, NY)
        total = part_v[mine, rows_of(low_x * PART + y_ * MAIN, MAIN), :]
        for d in range(1, NX):
            k = (d - 1) * NY + e
            arrived(xin_v.at[d - 1, e], rx.at[k])
            total = total + xin_v[d - 1, e]
        if e:
            ysend_v[e] = total
            send(ysend_v.at[e], yin_v.at[e], sy.at[e], ry.at[e], at(z, c, x, y_))
        else:
            kept = total
    rest = xsend2_v[mine, rows_of(low_x * REST, REST), :]
    for d in range(1, NX):
        arrived(xin2_v.at[d], rx2.at[d])
        rest = rest + xin2_v[d]
    for e in range(1, NY):
        arrived(yin_v.at[e], ry.at[e])
        kept = kept + yin_v[e]
    kept = jnp.concatenate([kept, rest], axis=0)
    arrived(backin_v, rf.at[0])
    done = -exact(kept + backin_v[...], unit_v[...])

    def main_rows(x_, y_):
        return out_v.at[x_ // 2, rows_of(lax.rem(x_, 2) * PART + y_ * MAIN, MAIN)]

    def rest_rows(x_, y_):
        return out_v.at[x_ // 2, rows_of(EDGE + y_ * 2 * REST + lax.rem(x_, 2) * REST, REST)]

    def rest_part(y_):
        return out_v.at[:, rows_of(EDGE + y_ * 2 * REST, 2 * REST)]

    main_rows(x, y)[...] = done[0:MAIN]
    rest_rows(x, y)[...] = done[MAIN:]
    for d in X_FAR:
        send(rest_rows(x, y), rest_rows(x, y), sxg2.at[d], rxg2.at[d], at(z, c, turn(x, d, NX), y))
    for e in Y_FAR:
        send(main_rows(x, y), main_rows(x, y), syg.at[e], ryg.at[e], at(z, c, x, turn(y, e, NY)))

    for e in (0,) + Y_NEAR:
        block = main_rows(x, turn(y, NY - e, NY))
        if e:
            arrived(block, ryg.at[e])
        for d in X_FAR:
            k = (d - 1) * NY + e
            send(block, block, sxg.at[k], rxg.at[k], at(z, c, turn(x, d, NX), y))
        if e == 1:
            for d in range(1, NX):
                arrived(rest_rows(turn(x, NX - d, NX), y), rxg2.at[d])
            for d in Y_FAR:
                send(rest_part(y), rest_part(y), syg2.at[d], ryg2.at[d], at(z, c, x, turn(y, d, NY)))

    for d in range(1, NX):
        for e in range(NY):
            arrived(main_rows(turn(x, NX - d, NX), turn(y, NY - e, NY)), rxg.at[(d - 1) * NY + e])
    for e in range(1, NY):
        arrived(rest_part(turn(y, NY - e, NY)), ryg2.at[e])

    def left_here(ref, sem):
        pltpu.make_async_copy(ref, ref, sem).wait()

    @pl.when(is_source)
    def _():
        for i in range((NZ - 1) * NC):
            left_here(relay_v.at[0], s1.at[i])

    @pl.when(has_block)
    def _():
        left_here(column_v, s3.at[0])

    for d in range(NX):
        x_ = turn(x, d, NX)

        @pl.when((2 * x_ + y // 4) != z)
        def _(d=d):
            for e in range(NC):
                if d or e:
                    left_here(relay_v.at[0], s2.at[d * NC + e])

    left_here(pairin_v, sp.at[0])
    for d in range(1, NZ):
        left_here(backs_v.at[d], sb.at[d])
    left_here(backsum_v, sf.at[0])
    for k in range((NX - 1) * NY):
        left_here(xin_v.at[0, 0], sx.at[k])
        left_here(xin_v.at[0, 0], sxg.at[k])
    for e in range(1, NY):
        left_here(yin_v.at[e], sy.at[e])
        left_here(yin_v.at[e], syg.at[e])
        left_here(yin2_v.at[e], sy2.at[e])
        left_here(yin2_v.at[e], syg2.at[e])
    for d in range(1, NX):
        left_here(xin2_v.at[d], sx2.at[d])
        left_here(xin2_v.at[d], sxg2.at[d])


def shards(strip, below, first, second, cotangent):
    f32, bf16 = jnp.float32, jnp.bfloat16
    dma = pltpu.SemaphoreType.DMA
    main = (NX - 1) * NY
    pairs = (
        (NZ - 1) * NC, NX, NX * NC, NX * NC, 1, 1, 1, 1, NZ, NZ, 1, 1,
        main, main, NY, NY, NY, NY, main, main,
        NY, NY, NX, NX, NX, NX, NY, NY,
    )
    out = pl.pallas_call(
        kernel,
        out_shape=pltpu.VMEM((2, HALF, STRIP), f32),
        in_specs=[pl.BlockSpec(memory_space=pltpu.HBM)] * 5,
        out_specs=pl.BlockSpec(memory_space=pltpu.VMEM),
        scratch_shapes=[
            pltpu.VMEM((ROWS, STRIP), f32),
            pltpu.VMEM((PANEL, PANEL), f32),
            pltpu.VMEM((PANEL, PANEL), f32),
            pltpu.VMEM((PANEL, PANEL), f32),
            pltpu.VMEM((ROWS, COLS), f32),
            pltpu.VMEM((ROWS, 2 * COLS), bf16),
            pltpu.VMEM((COLS, STRIP), f32),
            pltpu.VMEM((NX, PIECE, STRIP), f32),
            pltpu.VMEM((2 * COLS, 2 * STRIP), bf16),
            pltpu.VMEM((NC, NZ, SUB, STRIP), f32),
            pltpu.VMEM((NZ, SUB, STRIP), f32),
            pltpu.VMEM((NZ, SUB, STRIP), f32),
            pltpu.VMEM((SUB, STRIP), f32),
            pltpu.VMEM((SUB, STRIP), f32),
            pltpu.VMEM((2, HALF, STRIP), f32),
            pltpu.VMEM((NX - 1, NY, MAIN, STRIP), f32),
            pltpu.VMEM((NY, MAIN, STRIP), f32),
            pltpu.VMEM((NY, MAIN, STRIP), f32),
            pltpu.VMEM((NY, 2, 2 * REST, STRIP), f32),
            pltpu.VMEM((2, 2 * REST, STRIP), f32),
            pltpu.VMEM((NX, REST, STRIP), f32),
            pltpu.VMEM((STRIP, STRIP), f32),
            dma((4 + C_CHUNKS,)),
            pltpu.SemaphoreType.REGULAR,
        ] + [dma((n,)) for n in pairs],
        compiler_params=pltpu.CompilerParams(
            collective_id=0, has_side_effects=True, vmem_limit_bytes=40 << 20,
        ),
    )(*[pltpu.with_memory_space_constraint(v, pltpu.HBM) for v in (strip, below, first, second, cotangent)])
    return out.reshape(ROWS, STRIP)


def solution(mesh):
    return jax.shard_map(
        shards,
        mesh=mesh,
        in_specs=(P("row", None), P(), P(), P(), P("row", "col")),
        out_specs=P("row", None),
        check_vma=False,
    )
```

time: 67.1 us -> 58 us (0.86)
  local copies, waits for them, and re-layouts: 6.12 us -> 0.84 us
  Pallas kernels: 60.5 us -> 57.1 us
    unnamed x11 -> x1, local copies, waits for them, and re-layouts: 6.12 us -> 0.84 us
    pallas_call x1, Pallas kernels: 60.5 us -> 57.1 us  [shards(): pl.pallas_call(kernel, out_shape=pltpu.VMEM((2, HALF, STRIP), f32), in_sp...]
where the time goes in v2:
time: 58 us; the launch traced here: 57.9 us
  Pallas kernels  57.1 us (98%)
  local copies, waits for them, and re-layouts  0.84 us (1%)
    pallas_call x1, Pallas kernels, shards(): pl.pallas_call(kernel, out_shape=pltpu.VMEM((2, HALF, STRIP), f32), in_sp...  57.1 us

profile of v2, /device:TPU:1, one launch (start us, length us, event | category | flops | bytes accessed | tf_op | source)
XLA Modules:
  0.0 57.9 jit_solution(10876752318354452444)
XLA Ops:
  0.0 57.1 %shard_map.55 = f32[2,640,128]{2,1,0:T(8,128)S(1)} custom-call(f32[1280,128]{1,0:T(8,128)} %strip_h.1, f32[64,64]{1,0:T(8,128)} %below_h.1, f32[64,64]{1,0:T(8,128)} %first_h.1, f32[64,64]{1,0:T(8,128)} %second_h.1, f32[1280,640]{1,0:T(8,128)} %cot_h.1), custom_call_target="tpu_custom_call" | custom-call | tf_op jit(solution)/shard_map/pallas_call | solution.py:338
  57.1 0.8 %copy.7 = f32[1280,128]{1,0:T(8,128)} copy(f32[1280,128]{1,0:T(8,128)S(1)} %bitcast.1) | data formatting | bytes 1310720

commit v3 on v2

--- a/solution.py
+++ b/solution.py
@@ -40,7 +40,7 @@
 
 def kernel(
     strip_h, below_h, first_h, second_h, cot_h, out_v,
-    strip_v, below_v, first_v, second_v, cot_v, split_v, column_v, relay_v, weights_v,
+    strip_v, below_v, first_v, second_v, cot_v, split_v, column_v, weights_v,
     back_v, pairin_v, backs_v, backsum_v, backin_v,
     part_v, xin_v, ysend_v, yin_v, yin2_v, xsend2_v, xin2_v, unit_v,
     load_sem, peer_sem,
@@ -68,17 +68,28 @@
     def turn(base, d, n):
         return lax.rem(base + d, n)
 
+    is_source = (y // 2) == lax.rem(row, 4)
+    target_x = row // 4
+    source_rows = lax.rem(y, 2) * COLS
+    in_plane = (2 * x + y // 4) == z
+    has_block = jnp.logical_and(in_plane, lax.rem(y // 2, NC) == c)
+
     barrier = pltpu.get_barrier_semaphore()
-    peers = []
-    for d in range(1, NX):
-        peers += [at(z, c, turn(x, d, NX), y), at(z, 1 - c, turn(x, d, NX), y)]
-    for d in range(1, NY):
-        peers.append(at(z, c, x, turn(y, d, NY)))
-    for d in range(1, NZ):
-        peers += [at(turn(z, d, NZ), c, x, y), at(turn(z, d, NZ), 1 - c, x, y)]
-    peers.append(at(z, 1 - c, x, y))
+
+    def greet(peer):
+        pl.semaphore_signal(barrier, inc=1, device_id=peer, device_id_type=MESH)
+
+    @pl.when(jnp.logical_not(in_plane))
+    def _():
+        for x_ in range(NX):
+            greet(at(2 * x + y // 4, lax.rem(y // 2, NC), x_, y))
+
+    peers = [at(z, 1 - c, x, y)]
+    peers += [at(turn(z, d, NZ), c, x, y) for d in Z_FAR]
+    peers += [at(z, c, x, turn(y, d, NY)) for d in Y_FAR]
+    peers += [at(z, c, turn(x, d, NX), y) for d in X_FAR]
     for peer in peers:
-        pl.semaphore_signal(barrier, inc=1, device_id=peer, device_id_type=MESH)
+        greet(peer)
 
     small = []
     for i, (src, dst) in enumerate(((below_h, below_v), (first_h, first_v), (second_h, second_v), (strip_h, strip_v))):
@@ -93,22 +104,17 @@
         copy.start()
         loads.append(copy)
 
-    pl.semaphore_wait(barrier, len(peers))
+    pl.semaphore_wait(barrier, len(peers) + jnp.where(is_source, (NZ - 1) * NC, 0))
     for d in range(1, NX):
         pl.semaphore_signal(peer_sem, inc=1, device_id=at(z, c, turn(x, d, NX), y), device_id_type=MESH)
-
-    is_source = (y // 2) == lax.rem(row, 4)
-    target_x = row // 4
-    source_rows = lax.rem(y, 2) * COLS
-    in_plane = (2 * x + y // 4) == z
-    has_block = jnp.logical_and(in_plane, lax.rem(y // 2, NC) == c)
 
     @pl.when(is_source)
     def _():
         for i, d in enumerate(Z_FAR):
             for h in range(NC):
                 src = strip_h.at[rows_of(source_rows + (x * NC + h) * PIECE, PIECE)]
-                send(src, relay_v.at[target_x], s1.at[i * NC + h], r1.at[target_x], at(turn(z, d, NZ), h, x, y))
+                dst = column_v.at[rows_of((x * NC + h) * PIECE, PIECE)]
+                send(src, dst, s1.at[i * NC + h], r1.at[x], at(turn(z, d, NZ), h, target_x, y))
 
     @pl.when(has_block)
     def _():
@@ -144,20 +150,6 @@
     pl.semaphore_wait(peer_sem, NX - 1)
     send(back_v.at[1 - c], pairin_v, sp.at[0], rp.at[0], at(z, 1 - c, x, y))
 
-    for d in (1, 3, 2, 0):
-        x_ = turn(x, d, NX)
-
-        @pl.when((2 * x_ + y // 4) != z)
-        def _(d=d, x_=x_):
-            arrived(relay_v.at[x_], r1.at[x_])
-            here = rows_of((x * NC + c) * PIECE, PIECE)
-            for e in range(NC):
-                if d == 0 and e == 0:
-                    column_v[here, :] = relay_v[x_]
-                    continue
-                k = d * NC + e
-                send(relay_v.at[x_], column_v.at[here], s2.at[k], r2.at[x * NC + c], at(z, lax.rem(c + e, NC), x_, y))
-
     arrived(pairin_v, rp.at[0])
     back_v[c] = back_v[c] + pairin_v[...]
     for d in Z_FAR:
@@ -172,21 +164,33 @@
     def _():
         arrived(column_v, r3.at[0])
 
+    def lower_of(k):
+        start = k * PIECE
+        high, low = halves(exact(column_v[rows_of(start, PIECE), :], unit_v[...], ((1,), (1,))))
+        both = jnp.concatenate([high, low], axis=1)
+        weights_v[pl.ds(pl.multiple_of(start, 16), PIECE), :] = both
+        weights_v[pl.ds(pl.multiple_of(COLS + start, 16), PIECE), :] = both
+
     for d in (0, 1, 3, 2):
         x_ = turn(x, d, NX)
+        k = x_ * NC + c
 
         @pl.when(jnp.logical_not(in_plane))
-        def _(d=d, x_=x_):
-            for e in range(NC):
-                if d or e:
-                    k = x_ * NC + lax.rem(c + e, NC)
-                    arrived(column_v.at[rows_of(k * PIECE, PIECE)], r2.at[k])
-
-        start, size = x_ * (NC * PIECE), NC * PIECE
-        high, low = halves(exact(column_v[rows_of(start, size), :], unit_v[...], ((1,), (1,))))
-        both = jnp.concatenate([high, low], axis=1)
-        weights_v[pl.ds(pl.multiple_of(start, 32), size), :] = both
-        weights_v[pl.ds(pl.multiple_of(COLS + start, 32), size), :] = both
+        def _(d=d, x_=x_, k=k):
+            block = column_v.at[rows_of(k * PIECE, PIECE)]
+            arrived(block, r1.at[x_])
+            send(block, block, s2.at[d], r2.at[x_], at(z, 1 - c, x, y))
+
+        lower_of(k)
+    for d in (0, 1, 3, 2):
+        x_ = turn(x, d, NX)
+        k = x_ * NC + 1 - c
+
+        @pl.when(jnp.logical_not(in_plane))
+        def _(x_=x_, k=k):
+            arrived(column_v.at[rows_of(k * PIECE, PIECE)], r2.at[x_])
+
+        lower_of(k)
 
     def product(start, size):
         part = jnp.dot(
@@ -294,20 +298,16 @@
     @pl.when(is_source)
     def _():
         for i in range((NZ - 1) * NC):
-            left_here(relay_v.at[0], s1.at[i])
+            left_here(column_v.at[pl.ds(0, PIECE)], s1.at[i])
 
     @pl.when(has_block)
     def _():
         left_here(column_v, s3.at[0])
 
-    for d in range(NX):
-        x_ = turn(x, d, NX)
-
-        @pl.when((2 * x_ + y // 4) != z)
-        def _(d=d):
-            for e in range(NC):
-                if d or e:
-                    left_here(relay_v.at[0], s2.at[d * NC + e])
+    @pl.when(jnp.logical_not(in_plane))
+    def _():
+        for d in range(NX):
+            left_here(column_v.at[pl.ds(0, PIECE)], s2.at[d])
 
     left_here(pairin_v, sp.at[0])
     for d in range(1, NZ):
@@ -331,7 +331,7 @@
     dma = pltpu.SemaphoreType.DMA
     main = (NX - 1) * NY
     pairs = (
-        (NZ - 1) * NC, NX, NX * NC, NX * NC, 1, 1, 1, 1, NZ, NZ, 1, 1,
+        (NZ - 1) * NC, NX, NX, NX, 1, 1, 1, 1, NZ, NZ, 1, 1,
         main, main, NY, NY, NY, NY, main, main,
         NY, NY, NX, NX, NX, NX, NY, NY,
     )
@@ -348,7 +348,6 @@
             pltpu.VMEM((ROWS, COLS), f32),
             pltpu.VMEM((ROWS, 2 * COLS), bf16),
             pltpu.VMEM((COLS, STRIP), f32),
-            pltpu.VMEM((NX, PIECE, STRIP), f32),
             pltpu.VMEM((2 * COLS, 2 * STRIP), bf16),
             pltpu.VMEM((NC, NZ, SUB, STRIP), f32),
             pltpu.VMEM((NZ, SUB, STRIP), f32),

time: 58 us -> 55.3 us (0.953)
  Pallas kernels: 57.1 us -> 54.3 us
    pallas_call x1, Pallas kernels: 57.1 us -> 54.3 us  [shards(): pl.pallas_call(kernel, out_shape=pltpu.VMEM((2, HALF, STRIP), f32), in_sp...]
where the time goes in v3:
time: 55.3 us; the launch traced here: 55.2 us
  Pallas kernels  54.3 us (98%)
  local copies, waits for them, and re-layouts  0.84 us (2%)
    pallas_call x1, Pallas kernels, shards(): pl.pallas_call(kernel, out_shape=pltpu.VMEM((2, HALF, STRIP), f32), in_sp...  54.3 us

profile of v3, /device:TPU:1, one launch (start us, length us, event | category | flops | bytes accessed | tf_op | source)
XLA Modules:
  0.0 55.2 jit_solution(4472715890109957682)
XLA Ops:
  0.0 54.3 %shard_map.55 = f32[2,640,128]{2,1,0:T(8,128)S(1)} custom-call(f32[1280,128]{1,0:T(8,128)} %strip_h.1, f32[64,64]{1,0:T(8,128)} %below_h.1, f32[64,64]{1,0:T(8,128)} %first_h.1, f32[64,64]{1,0:T(8,128)} %second_h.1, f32[1280,640]{1,0:T(8,128)} %cot_h.1), custom_call_target="tpu_custom_call" | custom-call | tf_op jit(solution)/shard_map/pallas_call | solution.py:338
  54.3 0.8 %copy.7 = f32[1280,128]{1,0:T(8,128)} copy(f32[1280,128]{1,0:T(8,128)S(1)} %bitcast.1) | data formatting | bytes 1310720

commit v4 on v3

--- a/solution.py
+++ b/solution.py
@@ -108,17 +108,19 @@
     for d in range(1, NX):
         pl.semaphore_signal(peer_sem, inc=1, device_id=at(z, c, turn(x, d, NX), y), device_id_type=MESH)
 
+    small[3].wait()
+
     @pl.when(is_source)
     def _():
         for i, d in enumerate(Z_FAR):
             for h in range(NC):
-                src = strip_h.at[rows_of(source_rows + (x * NC + h) * PIECE, PIECE)]
+                src = strip_v.at[rows_of(source_rows + (x * NC + h) * PIECE, PIECE)]
                 dst = column_v.at[rows_of((x * NC + h) * PIECE, PIECE)]
                 send(src, dst, s1.at[i * NC + h], r1.at[x], at(turn(z, d, NZ), h, target_x, y))
 
     @pl.when(has_block)
     def _():
-        send(strip_h.at[rows_of(source_rows, COLS)], column_v, s3.at[0], r3.at[0], at(z, 1 - c, x, y))
+        send(strip_v.at[rows_of(source_rows, COLS)], column_v, s3.at[0], r3.at[0], at(z, 1 - c, x, y))
 
     for copy in small[:3]:
         copy.wait()
@@ -129,7 +131,6 @@
     unit_v[0:PANEL, PANEL:] = jnp.zeros_like(first)
     unit_v[PANEL:, 0:PANEL] = -mixed
     unit_v[PANEL:, PANEL:] = second
-    small[3].wait()
 
     for i in range(C_CHUNKS):
         loads[i].wait()
@@ -138,15 +139,18 @@
         split_v[rows, 0:COLS] = high
         split_v[rows, COLS:] = low
 
+    def piece_y(z_):
+        return lax.rem(y + z_ + (NZ + 4) - (2 * x + y // 4), NY)
+
     high, low = halves(jnp.transpose(exact(strip_v[...], unit_v[...], ((1,), (1,)))))
     back = jnp.dot(jnp.concatenate([high, low], axis=0), split_v[...], preferred_element_type=jnp.float32)
     back = back[0:STRIP] + back[STRIP:]
     back = jnp.transpose(back[:, 0:COLS] + back[:, COLS:])
     pieces = NZ * NC
     for k in range(pieces):
-        back_v[1 - k % 2, k // 2, 0:MAIN] = back[k * MAIN:(k + 1) * MAIN]
         rest = pieces * MAIN + (k % NY * 2 + k // NY) * REST
-        back_v[1 - k % 2, k // 2, MAIN:] = back[rest:rest + REST]
+        back_v[k // NY, k % NY, 0:MAIN] = back[k * MAIN:(k + 1) * MAIN]
+        back_v[k // NY, k % NY, MAIN:] = back[rest:rest + REST]
     pl.semaphore_wait(peer_sem, NX - 1)
     send(back_v.at[1 - c], pairin_v, sp.at[0], rp.at[0], at(z, 1 - c, x, y))
 
@@ -154,7 +158,7 @@
     back_v[c] = back_v[c] + pairin_v[...]
     for d in Z_FAR:
         z_ = turn(z, d, NZ)
-        send(back_v.at[c, z_], backs_v.at[d], sb.at[d], rb.at[d], at(z_, c, x, y))
+        send(back_v.at[c, piece_y(z_)], backs_v.at[d], sb.at[d], rb.at[d], at(z_, c, x, y))
 
     @pl.when(has_block)
     def _():
@@ -208,23 +212,24 @@
         x_ = turn(x, d, NX)
         half, start = x_ // 2, lax.rem(x_, 2) * PART
         part_v[half, rows_of(start, PART), :] = product(half * HALF + start, PART)
-        if d:
-            for e in Y_FAR + (0,):
-                y_ = turn(y, e, NY)
-                k = (d - 1) * NY + e
-                send(part_v.at[half, rows_of(start + y_ * MAIN, MAIN)], xin_v.at[d - 1, e], sx.at[k], rx.at[k], at(z, c, x_, y))
+    for e in Y_FAR + (0,):
+        y_ = turn(y, e, NY)
+        for d in X_FAR:
+            x_ = turn(x, d, NX)
+            k = (d - 1) * NY + e
+            src = part_v.at[x_ // 2, rows_of(lax.rem(x_, 2) * PART + y_ * MAIN, MAIN)]
+            send(src, xin_v.at[d - 1, e], sx.at[k], rx.at[k], at(z, c, x_, y))
 
     mine, low_x = x // 2, lax.rem(x, 2)
     kept = None
     for i, e in enumerate(Y_FAR + (0,)):
-        if i == 3:
-            total = back_v[c, z]
+        if i == 1:
+            total = back_v[c, piece_y(z)]
             for d in range(1, NZ):
                 arrived(backs_v.at[d], rb.at[d])
                 total = total + backs_v[d]
             backsum_v[...] = total
-            target = lax.rem(col, 2) * pieces + z * NC + (1 - c)
-            send(backsum_v, backin_v, sf.at[0], rf.at[0], (col // 2, target))
+            send(backsum_v, backin_v, sf.at[0], rf.at[0], at(2 * x + y // 4, lax.rem(y // 2, NC), lax.rem(y, 2) * 2 + c, piece_y(z)))
         if i == 6:
             total = part_v[:, rows_of(EDGE + y * 2 * REST, 2 * REST), :]
             for d in range(1, NY):
@@ -349,7 +354,7 @@
             pltpu.VMEM((ROWS, 2 * COLS), bf16),
             pltpu.VMEM((COLS, STRIP), f32),
             pltpu.VMEM((2 * COLS, 2 * STRIP), bf16),
-            pltpu.VMEM((NC, NZ, SUB, STRIP), f32),
+            pltpu.VMEM((NC, NY, SUB, STRIP), f32),
             pltpu.VMEM((NZ, SUB, STRIP), f32),
             pltpu.VMEM((NZ, SUB, STRIP), f32),
             pltpu.VMEM((SUB, STRIP), f32),

time: 55.3 us -> 50.8 us (0.919)
  Pallas kernels: 54.3 us -> 49.7 us
    pallas_call x1, Pallas kernels: 54.3 us -> 49.7 us  [shards(): pl.pallas_call(kernel, out_shape=pltpu.VMEM((2, HALF, STRIP), f32), in_sp...]
where the time goes in v4:
time: 50.8 us; the launch traced here: 50.5 us
  Pallas kernels  49.7 us (98%)
  local copies, waits for them, and re-layouts  0.84 us (2%)
    pallas_call x1, Pallas kernels, shards(): pl.pallas_call(kernel, out_shape=pltpu.VMEM((2, HALF, STRIP), f32), in_sp...  49.7 us

profile of v4, /device:TPU:1, one launch (start us, length us, event | category | flops | bytes accessed | tf_op | source)
XLA Modules:
  0.0 50.5 jit_solution(16695747516869604680)
XLA Ops:
  0.0 49.7 %shard_map.55 = f32[2,640,128]{2,1,0:T(8,128)S(1)} custom-call(f32[1280,128]{1,0:T(8,128)} %strip_h.1, f32[64,64]{1,0:T(8,128)} %below_h.1, f32[64,64]{1,0:T(8,128)} %first_h.1, f32[64,64]{1,0:T(8,128)} %second_h.1, f32[1280,640]{1,0:T(8,128)} %cot_h.1), custom_call_target="tpu_custom_call" | custom-call | tf_op jit(solution)/shard_map/pallas_call | solution.py:343
  49.7 0.8 %copy.7 = f32[1280,128]{1,0:T(8,128)} copy(f32[1280,128]{1,0:T(8,128)S(1)} %bitcast.1) | data formatting | bytes 1310720
